TPU v7x, 32 devices: a whole 2x2x4 slice. The times are simulated.
32 devices in a mesh: gx: 8 (over z, x), gy: 4 (over y, core).
Axes of the slice: x: 2, y: 2, z: 4, core: 2. Of those that a mesh axis runs over, the one named last changes fastest.
Arguments:
- tangent: float32 [128, 64, 512], P('gx', 'gy'), may hold values from -6 to 6
- hessian: bfloat16 [5, 5, 128, 64, 512], P(None, None, 'gx', 'gy'), may hold values from -1.5 to 8, as said below
- kernel_rows: float32 [5, 17], replicated, may hold values from -1 to 1
- kernel_cols: float32 [5, 17], replicated, may hold values from -1 to 1
- kernel_depth: bfloat16 [5, 17], replicated, may hold values from -1 to 1
Outputs:
- hessian_product: float32 [128, 64, 512], P('gx', 'gy')
Inputs may be any that keep to these rules, and one draw needn't show every extreme that they name: `hessian`: Off-diagonal entries lie within -1.5 to 1.5; diagonal entries are positive, between 0.3 and 8.
All inputs are finite; a program needn't handle non-finite values.
Results may differ from a plain program's by a relative error of at most 0.0022.
Values sent between devices are 32-bit elements; how exact they have to be, the bound alone decides.
A program may use at most 128 MiB of HBM per device.

v0:
```python
import jax
import jax.numpy as jnp
from jax import lax
from jax.experimental import pallas as pl
from jax.experimental.pallas import tpu as pltpu
from jax.sharding import PartitionSpec as P

RADIUS = 8
DENSITIES = 5
TAPS = 2 * RADIUS + 1
LANES = 128


def split(value):
    high = value.astype(jnp.bfloat16)
    low = (value - high.astype(jnp.float32)).astype(jnp.bfloat16)
    return high, low


def dot(left, right):
    return jnp.dot(left, right, preferred_element_type=jnp.float32)


def picked(taps, index):
    total = jnp.zeros(index.shape, jnp.float32)
    for tap in range(TAPS):
        weight = jnp.broadcast_to(taps[:, tap : tap + 1], index.shape)
        total = jnp.where(index == tap, weight, total)
    return total


def build_forward(sizes, pieces, rows, cols, by_row, by_col, packed_ref):
    span_rows, span_cols, ext_rows, ext_cols = sizes
    wide = ext_rows * ext_cols
    lane = lax.broadcasted_iota(jnp.int32, (span_rows, wide), 1)
    row_index = lane // ext_cols - lax.broadcasted_iota(jnp.int32, (span_rows, wide), 0)
    lane = lax.broadcasted_iota(jnp.int32, (span_cols, wide), 1)
    col_index = lane % ext_cols - lax.broadcasted_iota(jnp.int32, (span_cols, wide), 0)
    for a in range(DENSITIES):
        by_row[...] = picked(rows[a : a + 1], row_index)
        by_col[...] = picked(cols[a : a + 1], col_index)

        def body(r, carry):
            high, low = split(by_row[pl.ds(r, 1), :] * by_col[...])
            at = pl.ds(pl.multiple_of((a * span_rows + r) * span_cols, span_cols), span_cols)
            for offset, length, begin in pieces:
                for copy, value in enumerate((high, high, low)):
                    start = 3 * offset[0] + copy * offset[1] + offset[2]
                    packed_ref[at, start : start + length] = value[:, begin : begin + length]
            return carry

        lax.fori_loop(0, span_rows, body, 0)


def build_backward(sizes, rows, cols, by_row, by_col, high_ref, low_ref):
    span_rows, span_cols, ext_rows, ext_cols = sizes
    own = span_rows * span_cols
    lane = lax.broadcasted_iota(jnp.int32, (ext_rows, own), 1)
    row_index = lax.broadcasted_iota(jnp.int32, (ext_rows, own), 0) - lane // span_cols
    lane = lax.broadcasted_iota(jnp.int32, (ext_cols, own), 1)
    col_index = lax.broadcasted_iota(jnp.int32, (ext_cols, own), 0) - lane % span_cols
    for a in range(DENSITIES):
        by_row[:, a * own : (a + 1) * own] = picked(rows[a : a + 1], row_index)
        by_col[:, a * own : (a + 1) * own] = picked(cols[a : a + 1], col_index)

    def body(r, carry):
        high, low = split(by_row[pl.ds(r, 1), :] * by_col[...])
        start = pl.multiple_of(r * ext_cols, ext_cols)
        high_ref[pl.ds(start, ext_cols), :] = high
        low_ref[pl.ds(start, ext_cols), :] = low
        return carry

    lax.fori_loop(0, ext_rows, body, 0)


def build_bands(depth_taps, band_ref):
    depth = band_ref.shape[1]
    blocks = depth // LANES
    shape = (LANES, LANES)
    index = lax.broadcasted_iota(jnp.int32, shape, 0) - lax.broadcasted_iota(jnp.int32, shape, 1) + RADIUS
    for a in range(DENSITIES):
        taps = depth_taps[a : a + 1]
        same = picked(taps, index).astype(jnp.bfloat16)
        after = picked(taps, index - LANES).astype(jnp.bfloat16)
        before = picked(taps, index + LANES).astype(jnp.bfloat16)
        for p in range(blocks):
            for q in range(blocks):
                block = {0: same, 1: after, -1: before}.get(q - p, jnp.zeros(shape, jnp.bfloat16))
                band_ref[a, p * LANES : (p + 1) * LANES, q * LANES : (q + 1) * LANES] = block


def compute(sizes, counts, tangent_ref, hess_ref, rows_ref, cols_ref, depth_ref, out_ref,
            ext, parts, by_row, by_col, by_row_t, by_col_t, fwd, bwd_high, bwd_low,
            bands, hess, lowered, acc, dens, back_high, back_low, spread, from_left, from_right,
            from_up, from_down, local_sems, send_sems, recv_sems, back_send_sems, back_recv_sems):
    span_rows, span_cols, ext_rows, ext_cols = sizes
    depth = acc.shape[1]
    reach = RADIUS
    own, wide = span_rows * span_cols, ext_rows * ext_cols
    edge, inner = reach * ext_cols, span_rows * ext_cols
    pieces = (((0, inner, 0), inner, edge), ((inner, 2 * edge, 0), edge, 0),
              ((inner, 2 * edge, edge), edge, edge + inner))
    gx, gy = lax.axis_index("gx"), lax.axis_index("gy")
    up = {"gx": lax.rem(gx + counts[0] - 1, counts[0])}
    down = {"gx": lax.rem(gx + 1, counts[0])}
    left = {"gy": lax.rem(gy + counts[1] - 1, counts[1])}
    right = {"gy": lax.rem(gy + 1, counts[1])}
    mesh_ids = pl.DeviceIdType.MESH

    fetch = pltpu.make_async_copy(hess_ref, hess, local_sems.at[0])
    fetch.start()
    inner_rows, inner_cols = pl.ds(reach, span_rows), pl.ds(reach, span_cols)
    home = pltpu.make_async_copy(tangent_ref, ext.at[inner_rows, inner_cols, :], local_sems.at[1])
    home.start()

    barrier = pltpu.get_barrier_semaphore()
    for neighbour in (up, down, left, right):
        pl.semaphore_signal(barrier, inc=1, device_id=neighbour, device_id_type=mesh_ids)
    pl.semaphore_wait(barrier, 4)

    first, last = pl.ds(0, reach), pl.ds(reach + span_rows, reach)
    first_cols, last_cols = pl.ds(0, reach), pl.ds(reach + span_cols, reach)
    chunks = depth // LANES
    lanes = [pl.ds(c * LANES, LANES) for c in range(chunks)]

    def remote(source, target, send_sem, recv_sem, device):
        return pltpu.make_async_remote_copy(
            src_ref=source, dst_ref=target, send_sem=send_sem, recv_sem=recv_sem,
            device_id=device, device_id_type=mesh_ids)

    head_rows, tail_rows = pl.ds(0, reach), pl.ds(span_rows - reach, reach)
    head_cols, tail_cols = pl.ds(0, reach), pl.ds(span_cols - reach, reach)
    copies = {}
    for c in range(chunks):
        z = lanes[c]
        every_row, every_col = pl.ds(0, span_rows), pl.ds(0, span_cols)
        plan = [
            (tangent_ref.at[tail_rows, every_col, z], ext.at[first, inner_cols, z], down),
            (tangent_ref.at[head_rows, every_col, z], ext.at[last, inner_cols, z], up),
            (tangent_ref.at[every_row, tail_cols, z], ext.at[inner_rows, first_cols, z], right),
            (tangent_ref.at[every_row, head_cols, z], ext.at[inner_rows, last_cols, z], left),
        ]
        near_last, near_first = pl.ds(span_cols, reach), pl.ds(reach, reach)
        for rows_at in (first, last):
            plan.append((ext.at[rows_at, near_last, z], ext.at[rows_at, first_cols, z], right))
            plan.append((ext.at[rows_at, near_first, z], ext.at[rows_at, last_cols, z], left))
        for kind, (source, target, device) in enumerate(plan):
            copies[kind, c] = remote(source, target, send_sems.at[kind, c], recv_sems.at[kind, c], device)
    for c in range(chunks):
        for kind in range(4):
            copies[kind, c].start()

    def relay(c):
        for kind in (0, 1):
            copies[kind, c].wait_recv()
        for kind in (4, 5, 6, 7):
            copies[kind, c].start()

    rows, cols = rows_ref[...], cols_ref[...]
    build_forward(sizes, pieces, rows, cols, by_row, by_col, fwd)
    build_bands(depth_ref[...].astype(jnp.float32), bands)
    build_backward(sizes, rows, cols, by_row_t, by_col_t, bwd_high, bwd_low)
    home.wait()

    halves = max(1, depth // 256)
    half = depth // halves
    per_half = chunks // halves

    def prepare(z, piece):
        offset, length, begin = piece
        block = ext[pl.ds(begin // ext_cols, length // ext_cols), :, z].reshape(length, z.size)
        high, low = split(block)
        for copy, value in enumerate((high, low, high)):
            parts[pl.ds(3 * offset[0] + copy * offset[1] + offset[2], length), z] = value

    def lateral(z, start, length, fresh):
        def body(a, carry):
            part = pl.ds(pl.multiple_of(a * own, own), own)
            total = dot(fwd[part, pl.ds(start, length)], parts[pl.ds(start, length), z])
            acc[part, z] = total if fresh else acc[part, z] + total
            return carry

        lax.fori_loop(0, DENSITIES, body, 0)

    def middle(h):
        for c in range(h * per_half, (h + 1) * per_half):
            copies[2, c].wait_recv()
            copies[3, c].wait_recv()
        z = pl.ds(h * half, half)
        prepare(z, pieces[0])
        lateral(z, 0, 3 * inner, True)

    def edges(begin, end):
        for c in range(begin, end):
            for kind in (4, 5, 6, 7):
                copies[kind, c].wait_recv()
        z = pl.ds(begin * LANES, (end - begin) * LANES)
        prepare(z, pieces[1])
        prepare(z, pieces[2])
        lateral(z, 3 * inner, 6 * edge, False)

    def along_depth(source, target):
        def body(a, carry):
            part = pl.ds(pl.multiple_of(a * own, own), own)
            dens[part, target] = dot(acc[part, source].astype(jnp.bfloat16), bands[a, source, target])
            return carry

        lax.fori_loop(0, DENSITIES, body, 0)

    def gradient(middle_lanes, source, target):
        step = 16

        def piece(i, carry):
            at = pl.ds(pl.multiple_of(i * step, step), step)
            for lane in range(middle_lanes.start, middle_lanes.start + middle_lanes.size, LANES):
                z = pl.ds(lane, LANES)
                values = [dens[pl.ds(pl.multiple_of(b * own + i * step, step), step), z]
                          for b in range(DENSITIES)]
                for a in range(DENSITIES):
                    total = None
                    for b in range(DENSITIES):
                        term = hess[a, b, at, z].astype(jnp.float32) * values[b]
                        total = term if total is None else total + term
                    into = pl.ds(pl.multiple_of(a * own + i * step, step), step)
                    lowered[into, z] = total.astype(jnp.bfloat16)
            return carry

        lax.fori_loop(0, own // step, piece, 0)

        def body(a, carry):
            part = pl.ds(pl.multiple_of(a * own, own), own)
            back = lax.dot_general(lowered[part, source], bands[a, target, source],
                                   (((1,), (1,)), ((), ())), preferred_element_type=jnp.float32)
            back_high[part, target], back_low[part, target] = split(back)
            return carry

        lax.fori_loop(0, DENSITIES, body, 0)

    def contribute(h, start, count):
        z = pl.ds(h * half, half)
        at = pl.ds(start * ext_cols, count * ext_cols)
        lead = bwd_high[at, :]
        flat = dot(lead, back_high[:, z]) + dot(lead, back_low[:, z]) + dot(bwd_low[at, :], back_high[:, z])
        spread[pl.ds(start, count), :, z] = flat.reshape(count, ext_cols, half)

    returns = {}
    for h in range(halves):
        z = pl.ds(h * half, half)
        plan = []
        for rows_at in (first, last, inner_rows):
            plan.append((spread.at[rows_at, last_cols, z], from_left.at[rows_at, :, z], right))
            plan.append((spread.at[rows_at, first_cols, z], from_right.at[rows_at, :, z], left))
        plan.append((spread.at[first, inner_cols, z], from_down.at[:, :, z], up))
        plan.append((spread.at[last, inner_cols, z], from_up.at[:, :, z], down))
        for kind, (source, target, device) in enumerate(plan):
            returns[kind, h] = remote(source, target, back_send_sems.at[kind, h], back_recv_sems.at[kind, h], device)

    def strips(h):
        z = pl.ds(h * half, half)
        for kind, rows_at, strip in ((0, first, 6), (2, last, 7)):
            returns[kind, h].wait_recv()
            returns[kind + 1, h].wait_recv()
            near = pl.ds(reach, reach)
            spread[rows_at, near, z] = spread[rows_at, near, z] + from_left[rows_at, :, z]
            far = pl.ds(span_cols, reach)
            spread[rows_at, far, z] = spread[rows_at, far, z] + from_right[rows_at, :, z]
            returns[strip, h].start()

    def corners(h):
        contribute(h, 0, reach)
        for kind in (0, 1):
            returns[kind, h].start()
        contribute(h, reach + span_rows, reach)
        for kind in (2, 3):
            returns[kind, h].start()

    def sides(h):
        for start in range(reach, reach + span_rows, reach):
            contribute(h, start, reach)
        for kind in (4, 5):
            returns[kind, h].start()

    relayed = 0
    for h in range(halves):
        middle(h)
        if relayed < chunks:
            relay(relayed)
            relayed += 1
    while relayed < chunks:
        relay(relayed)
        relayed += 1
    for h in range(halves):
        edges(h * per_half, (h + 1) * per_half)
    every = pl.ds(0, depth)
    along_depth(every, every)
    fetch.wait()
    gradient(every, every, every)
    for h in range(halves):
        corners(h)
    for h in range(halves):
        strips(h)
    for h in range(halves):
        sides(h)
    for h in range(halves):
        z = pl.ds(h * half, half)
        for kind in (4, 5):
            returns[kind, h].wait_recv()
        out_ref[:, :, z] = spread[inner_rows, inner_cols, z]
        out_ref[:, head_cols, z] = out_ref[:, head_cols, z] + from_left[inner_rows, :, z]
        out_ref[:, tail_cols, z] = out_ref[:, tail_cols, z] + from_right[inner_rows, :, z]
        for kind in (6, 7):
            returns[kind, h].wait_recv()
        out_ref[head_rows, :, z] = out_ref[head_rows, :, z] + from_up[:, :, z]
        out_ref[tail_rows, :, z] = out_ref[tail_rows, :, z] + from_down[:, :, z]
    for copy in list(copies.values()) + list(returns.values()):
        copy.wait_send()


def per_device(tangent, hessian, kernel_rows, kernel_cols, kernel_depth):
    span_rows, span_cols, depth = tangent.shape
    reach = RADIUS
    ext_rows, ext_cols = span_rows + 2 * reach, span_cols + 2 * reach
    sizes = (span_rows, span_cols, ext_rows, ext_cols)
    counts = (lax.axis_size("gx"), lax.axis_size("gy"))
    own, wide = span_rows * span_cols, ext_rows * ext_cols
    chunks, halves = depth // LANES, max(1, depth // 256)
    full = pl.BlockSpec(memory_space=pltpu.VMEM)
    anywhere = pl.BlockSpec(memory_space=pl.ANY)
    bf16, f32 = jnp.bfloat16, jnp.float32
    return pl.pallas_call(
        lambda *refs: compute(sizes, counts, *refs),
        out_shape=jax.ShapeDtypeStruct((span_rows, span_cols, depth), f32),
        in_specs=[anywhere, anywhere, full, full, full],
        out_specs=full,
        scratch_shapes=[
            pltpu.VMEM((ext_rows, ext_cols, depth), f32),
            pltpu.VMEM((3 * wide, depth), bf16),
            pltpu.VMEM((span_rows, wide), f32),
            pltpu.VMEM((span_cols, wide), f32),
            pltpu.VMEM((ext_rows, DENSITIES * own), f32),
            pltpu.VMEM((ext_cols, DENSITIES * own), f32),
            pltpu.VMEM((DENSITIES * own, 3 * wide), bf16),
            pltpu.VMEM((wide, DENSITIES * own), bf16),
            pltpu.VMEM((wide, DENSITIES * own), bf16),
            pltpu.VMEM((DENSITIES, depth, depth), bf16),
            pltpu.VMEM((DENSITIES, DENSITIES, own, depth), bf16),
            pltpu.VMEM((DENSITIES * own, depth), bf16),
            pltpu.VMEM((DENSITIES * own, depth), f32),
            pltpu.VMEM((DENSITIES * own, depth), f32),
            pltpu.VMEM((DENSITIES * own, depth), bf16),
            pltpu.VMEM((DENSITIES * own, depth), bf16),
            pltpu.VMEM((ext_rows, ext_cols, depth), f32),
            pltpu.VMEM((ext_rows, reach, depth), f32),
            pltpu.VMEM((ext_rows, reach, depth), f32),
            pltpu.VMEM((reach, span_cols, depth), f32),
            pltpu.VMEM((reach, span_cols, depth), f32),
            pltpu.SemaphoreType.DMA((2,)),
            pltpu.SemaphoreType.DMA((8, chunks)),
            pltpu.SemaphoreType.DMA((8, chunks)),
            pltpu.SemaphoreType.DMA((8, halves)),
            pltpu.SemaphoreType.DMA((8, halves)),
        ],
        compiler_params=pltpu.CompilerParams(
            vmem_limit_bytes=60 << 20, collective_id=0, has_side_effects=True),
    )(tangent, hessian.reshape(DENSITIES, DENSITIES, own, depth), kernel_rows, kernel_cols, kernel_depth)


def solution(mesh):
    return jax.shard_map(
        per_device,
        mesh=mesh,
        in_specs=(P("gx", "gy", None), P(None, None, "gx", "gy", None), P(), P(), P()),
        out_specs=P("gx", "gy", None),
        check_vma=False,
    )
```

profile of v0, /device:TPU:0, one launch (start us, length us, event | category | flops | bytes accessed | tf_op | source)
XLA Modules:
  0.0 50.2 jit_solution(13401645869290446771)
XLA Ops:
  0.0 48.3 %shard_map.55 = f32[16,16,512]{2,1,0:T(8,128)} custom-call(f32[16,16,512]{2,1,0:T(8,128)} %refs_0_.1, bf16[5,5,256,512]{3,2,1,0:T(8,128)(2,1)} %bitcast.1, f32[5,17]{1,0:T(8,128)} %refs_2_.1, f32[5,17]{1,0:T(8,128)} %refs_3_.1, bf16[5,17]{1,0:T(8,128)(2,1)} %refs_4_.1), custom_call_target="tpu_custom_call" | custom-call | tf_op jit(solution)/shard_map/pallas_call | solution.py:330
  48.3 1.9 %copy.7 = f32[16,16,512]{2,1,0:T(8,128)} copy(f32[16,16,512]{2,1,0:T(8,128)} %shard_map.55) | data formatting | bytes 1048576
where the time goes:
time: 50.3 us; the launch traced here: 50.2 us
  Pallas kernels  48.3 us (96%)
  local copies, waits for them, and re-layouts  1.88 us (4%)
    pallas_call x1, Pallas kernels, per_device(): pl.pallas_call(lambda *refs: compute(sizes, counts, *refs), out_shape=jax...  48.3 us
    unnamed x1, local copies, waits for them, and re-layouts  1.88 us

commit v1 on v0

v1 whole, which is shorter than its diff:
```python
import jax
import jax.numpy as jnp
from jax import lax
from jax.experimental import pallas as pl
from jax.experimental.pallas import tpu as pltpu
from jax.sharding import PartitionSpec as P

RADIUS = 8
DENSITIES = 5
TAPS = 2 * RADIUS + 1
LANES = 128
WINDOW = 2 * LANES


def split(value):
    high = value.astype(jnp.bfloat16)
    low = (value - high.astype(jnp.float32)).astype(jnp.bfloat16)
    return high, low


def dot(left, right):
    return jnp.dot(left, right, preferred_element_type=jnp.float32)


def dot3(left_high, left_low, right_high, right_low):
    return dot(left_high, right_high) + dot(left_high, right_low) + dot(left_low, right_high)


def picked(taps, index):
    total = jnp.zeros(index.shape, jnp.float32)
    for tap in range(TAPS):
        weight = jnp.broadcast_to(taps[:, tap : tap + 1], index.shape)
        total = jnp.where(index == tap, weight, total)
    return total


def iota(shape, axis):
    return lax.broadcasted_iota(jnp.int32, shape, axis)


def build_forward(sizes, rows, cols, high_ref, low_ref):
    span_cols, ext_cols = sizes[1], sizes[3]
    wide = 3 * RADIUS * ext_cols
    row_index = iota((RADIUS, wide), 1) // ext_cols - iota((RADIUS, wide), 0)
    col_index = iota((span_cols, LANES), 1) % ext_cols - iota((span_cols, LANES), 0)
    for a in range(DENSITIES):
        by_row = picked(rows[a : a + 1], row_index)
        by_col = picked(cols[a : a + 1], col_index)
        by_col = jnp.concatenate([by_col] * (wide // LANES), axis=1)
        for r in range(RADIUS):
            at = pl.ds((a * RADIUS + r) * span_cols, span_cols)
            high_ref[at, :], low_ref[at, :] = split(by_row[r : r + 1, :] * by_col)


def build_backward(sizes, rows, cols, high_ref, low_ref):
    span_cols, ext_cols = sizes[1], sizes[3]
    size = RADIUS * span_cols
    row_index = iota((3 * RADIUS, size), 0) - iota((3 * RADIUS, size), 1) // span_cols
    col_index = iota((ext_cols, size), 0) - iota((ext_cols, size), 1) % span_cols
    for a in range(DENSITIES):
        by_row = picked(rows[a : a + 1], row_index)
        by_col = picked(cols[a : a + 1], col_index)
        into = pl.ds(a * size, size)
        for r in range(3 * RADIUS):
            at = pl.ds(r * ext_cols, ext_cols)
            high_ref[at, into], low_ref[at, into] = split(by_row[r : r + 1, :] * by_col)


def build_bands(depth_taps, band_ref, band_t_ref):
    step = 16
    shape = (step, WINDOW)
    offset = iota(shape, 0) - iota(shape, 1)
    for a in range(DENSITIES):
        taps = depth_taps[a : a + 1]
        for ref, sign in ((band_ref, 1), (band_t_ref, -1)):
            middle = picked(taps, sign * (offset + LANES) + RADIUS)
            for i in range(WINDOW // step):
                value = pltpu.roll(middle, (step * i - LANES) % WINDOW, 1)
                if i in (0, WINDOW // step - 1):
                    value = jnp.where(jnp.abs(offset + step * i) <= RADIUS, value, 0.0)
                ref[a, pl.ds(i * step, step), :] = value.astype(jnp.bfloat16)


def compute(sizes, counts, tangent_ref, hess_ref, rows_ref, cols_ref, depth_ref, out_ref,
            ext, high, low, fwd_high, fwd_low, bwd_high, bwd_low, band, band_t, hess,
            acc, lateral, dens, lowered, pending, back_high, back_low, spread,
            from_left, from_right, from_up, from_down,
            local_sems, out_sems, send_sems, recv_sems, back_send_sems, back_recv_sems):
    span_rows, span_cols, ext_rows, ext_cols = sizes
    depth = acc.shape[-1]
    reach = RADIUS
    groups = span_rows // reach
    own, size, block = span_rows * span_cols, reach * span_cols, reach * ext_cols
    chunks = depth // LANES
    gx, gy = lax.axis_index("gx"), lax.axis_index("gy")
    up = {"gx": lax.rem(gx + counts[0] - 1, counts[0])}
    down = {"gx": lax.rem(gx + 1, counts[0])}
    left = {"gy": lax.rem(gy + counts[1] - 1, counts[1])}
    right = {"gy": lax.rem(gy + 1, counts[1])}
    mesh_ids = pl.DeviceIdType.MESH

    inner_rows, inner_cols = pl.ds(reach, span_rows), pl.ds(reach, span_cols)
    barrier = pltpu.get_barrier_semaphore()
    for neighbour in (up, down, left, right):
        pl.semaphore_signal(barrier, inc=1, device_id=neighbour, device_id_type=mesh_ids)
    fetch = pltpu.make_async_copy(hess_ref, hess, local_sems.at[0])
    home = pltpu.make_async_copy(tangent_ref, ext.at[inner_rows, inner_cols, :], local_sems.at[1])
    home.start()
    pl.semaphore_wait(barrier, 4)

    first, last = pl.ds(0, reach), pl.ds(reach + span_rows, reach)
    first_cols, last_cols = pl.ds(0, reach), pl.ds(reach + span_cols, reach)
    near_first, near_last = pl.ds(reach, reach), pl.ds(span_cols, reach)
    lanes = [pl.ds(c * LANES, LANES) for c in range(chunks)]

    def remote(source, target, send_sem, recv_sem, device):
        return pltpu.make_async_remote_copy(
            src_ref=source, dst_ref=target, send_sem=send_sem, recv_sem=recv_sem,
            device_id=device, device_id_type=mesh_ids)

    head_rows, tail_rows = pl.ds(0, reach), pl.ds(span_rows - reach, reach)
    head_cols, tail_cols = pl.ds(0, reach), pl.ds(span_cols - reach, reach)
    every_row, every_col = pl.ds(0, span_rows), pl.ds(0, span_cols)
    copies, returns = {}, {}
    for c, z in enumerate(lanes):
        plan = [
            (tangent_ref.at[tail_rows, every_col, z], ext.at[first, inner_cols, z], down),
            (tangent_ref.at[head_rows, every_col, z], ext.at[last, inner_cols, z], up),
            (tangent_ref.at[every_row, tail_cols, z], ext.at[inner_rows, first_cols, z], right),
            (tangent_ref.at[every_row, head_cols, z], ext.at[inner_rows, last_cols, z], left),
        ]
        for rows_at in (first, last):
            plan.append((ext.at[rows_at, near_last, z], ext.at[rows_at, first_cols, z], right))
            plan.append((ext.at[rows_at, near_first, z], ext.at[rows_at, last_cols, z], left))
        for kind, (source, target, device) in enumerate(plan):
            copies[kind, c] = remote(source, target, send_sems.at[kind, c], recv_sems.at[kind, c], device)
        plan = []
        for rows_at in (first, last, inner_rows):
            plan.append((spread.at[rows_at, last_cols, z], from_left.at[rows_at, :, z], right))
            plan.append((spread.at[rows_at, first_cols, z], from_right.at[rows_at, :, z], left))
        plan.append((spread.at[first, inner_cols, z], from_down.at[:, :, z], up))
        plan.append((spread.at[last, inner_cols, z], from_up.at[:, :, z], down))
        for kind, (source, target, device) in enumerate(plan):
            returns[kind, c] = remote(source, target, back_send_sems.at[kind, c], back_recv_sems.at[kind, c], device)
    for c in range(chunks):
        for kind in range(4):
            copies[kind, c].start()
    fetch.start()

    def relay(c):
        for kind in (0, 1):
            copies[kind, c].wait_recv()
        for kind in (4, 5, 6, 7):
            copies[kind, c].start()

    def prepare(z, begin, count):
        value = ext[pl.ds(begin * reach, count * reach), :, z].reshape(count * block, z.size)
        at = pl.ds(begin * block, count * block)
        high[at, z], low[at, z] = split(value)

    def product(group, begin, end, z):
        weights, data = pl.ds((begin - group) * block, (end - begin) * block), pl.ds(begin * block, (end - begin) * block)
        return dot3(fwd_high[:, weights], fwd_low[:, weights], high[data, z], low[data, z])

    def middle(begin, end):
        z = pl.ds(begin * LANES, (end - begin) * LANES)
        for c in range(begin, end):
            copies[2, c].wait_recv()
            copies[3, c].wait_recv()
        prepare(z, 1, groups)
        for group in range(groups):
            acc[group, :, z] = product(group, max(group, 1), min(group + 3, groups + 1), z)

    def edges(begin, end):
        z = pl.ds(begin * LANES, (end - begin) * LANES)
        for c in range(begin, end):
            for kind in (4, 5, 6, 7):
                copies[kind, c].wait_recv()
        prepare(z, 0, 1)
        prepare(z, groups + 1, 1)
        for group in range(groups):
            total = acc[group, :, z]
            if group == 0:
                total = total + product(group, 0, 1, z)
            if group == groups - 1:
                total = total + product(group, groups + 1, groups + 2, z)
            total = total.astype(jnp.bfloat16)
            for a in range(DENSITIES):
                lateral[a, pl.ds(group * size, size), z] = total[a * size : (a + 1) * size]

    keep = iota((own, LANES), 1) < LANES // 2

    def along_depth(k):
        z, here, ahead = pl.ds(k * LANES, WINDOW), lanes[k], lanes[k + 1]
        for a in range(DENSITIES):
            value = dot(lateral[a, :, z], band[a])
            begin = value[:, :LANES]
            dens[a, :, here] = begin if k == 0 else jnp.where(keep, dens[a, :, here], begin)
            dens[a, :, ahead] = value[:, LANES:]

    def gradient(k):
        step = 16

        def piece(i, carry):
            at = pl.ds(pl.multiple_of(i * step, step), step)
            for z in (lanes[k], lanes[k + 1]):
                values = [dens[b, at, z] for b in range(DENSITIES)]
                for a in range(DENSITIES):
                    total = None
                    for b in range(DENSITIES):
                        term = hess[a, b, at, z].astype(jnp.float32) * values[b]
                        total = term if total is None else total + term
                    lowered[a, at, z] = total.astype(jnp.bfloat16)
            return carry

        lax.fori_loop(0, own // step, piece, 0)

    def against_depth(k):
        z, here, ahead = pl.ds(k * LANES, WINDOW), lanes[k], lanes[k + 1]

        def finish(a, value, target):
            value_high, value_low = split(value)
            for group in range(groups):
                part = pl.ds(a * size, size)
                back_high[group, part, target] = value_high[group * size : (group + 1) * size]
                back_low[group, part, target] = value_low[group * size : (group + 1) * size]

        for a in range(DENSITIES):
            value = dot(lowered[a, :, z], band_t[a])
            begin = value[:, :LANES]
            finish(a, begin if k == 0 else jnp.where(keep, pending[a], begin), here)
            if k == chunks - 2:
                finish(a, value[:, LANES:], ahead)
            else:
                pending[a] = value[:, LANES:]

    def spread_block(index, z):
        total = None
        for group in range(groups):
            if 0 <= index - group < 3:
                part = pl.ds((index - group) * block, block)
                term = dot3(bwd_high[part, :], bwd_low[part, :], back_high[group, :, z], back_low[group, :, z])
                total = term if total is None else total + term
        spread[pl.ds(index * reach, reach), :, z] = total.reshape(reach, ext_cols, z.size)

    def corners(begin, end):
        z = pl.ds(begin * LANES, (end - begin) * LANES)
        spread_block(0, z)
        spread_block(groups + 1, z)
        for c in range(begin, end):
            for kind in (0, 1, 2, 3):
                returns[kind, c].start()

    def sides(begin, end):
        z = pl.ds(begin * LANES, (end - begin) * LANES)
        for index in range(1, groups + 1):
            spread_block(index, z)
        for c in range(begin, end):
            for kind in (4, 5):
                returns[kind, c].start()

    def strips(c):
        z = lanes[c]
        for kind, rows_at, strip in ((0, first, 6), (2, last, 7)):
            returns[kind, c].wait_recv()
            returns[kind + 1, c].wait_recv()
            spread[rows_at, near_first, z] = spread[rows_at, near_first, z] + from_left[rows_at, :, z]
            spread[rows_at, near_last, z] = spread[rows_at, near_last, z] + from_right[rows_at, :, z]
            returns[strip, c].start()

    def final(c):
        z = lanes[c]
        for kind in (4, 5, 6, 7):
            returns[kind, c].wait_recv()
        spread[inner_rows, near_first, z] = spread[inner_rows, near_first, z] + from_left[inner_rows, :, z]
        spread[inner_rows, near_last, z] = spread[inner_rows, near_last, z] + from_right[inner_rows, :, z]
        top, bottom = pl.ds(reach, reach), pl.ds(span_rows, reach)
        spread[top, inner_cols, z] = spread[top, inner_cols, z] + from_up[:, :, z]
        spread[bottom, inner_cols, z] = spread[bottom, inner_cols, z] + from_down[:, :, z]
        copy = pltpu.make_async_copy(spread.at[inner_rows, inner_cols, z], out_ref.at[:, :, z], out_sems.at[c])
        copy.start()
        return copy

    rows, cols = rows_ref[...], cols_ref[...]
    build_forward(sizes, rows, cols, fwd_high, fwd_low)
    build_bands(depth_ref[...].astype(jnp.float32), band, band_t)
    build_backward(sizes, rows, cols, bwd_high, bwd_low)
    home.wait()
    relay(0)
    middle(0, 2)
    relay(1)
    for c in range(2, chunks, 2):
        middle(c, min(c + 2, chunks))
    edges(0, 2)
    relayed = 2
    fetch.wait()
    for k in range(chunks - 1):
        if k > 0:
            edges(k + 1, k + 2)
        if relayed < chunks:
            relay(relayed)
            relayed += 1
        along_depth(k)
        gradient(k)
        if k > 0:
            strips(k - 1)
        against_depth(k)
        final_step = k == chunks - 2
        corners(k, chunks if final_step else k + 1)
        if relayed < chunks:
            relay(relayed)
            relayed += 1
        sides(k, chunks if final_step else k + 1)
    strips(chunks - 2)
    strips(chunks - 1)
    outs = [final(c) for c in range(chunks)]
    for copy in list(copies.values()) + list(returns.values()):
        copy.wait_send()
    for copy in outs:
        copy.wait()


def per_device(tangent, hessian, kernel_rows, kernel_cols, kernel_depth):
    span_rows, span_cols, depth = tangent.shape
    reach = RADIUS
    ext_rows, ext_cols = span_rows + 2 * reach, span_cols + 2 * reach
    sizes = (span_rows, span_cols, ext_rows, ext_cols)
    counts = (lax.axis_size("gx"), lax.axis_size("gy"))
    own, wide = span_rows * span_cols, ext_rows * ext_cols
    groups, size, block = span_rows // reach, reach * span_cols, reach * ext_cols
    chunks = depth // LANES
    full = pl.BlockSpec(memory_space=pltpu.VMEM)
    anywhere = pl.BlockSpec(memory_space=pl.ANY)
    bf16, f32 = jnp.bfloat16, jnp.float32
    return pl.pallas_call(
        lambda *refs: compute(sizes, counts, *refs),
        out_shape=jax.ShapeDtypeStruct((span_rows, span_cols, depth), f32),
        in_specs=[anywhere, anywhere, full, full, full],
        out_specs=anywhere,
        scratch_shapes=[
            pltpu.VMEM((ext_rows, ext_cols, depth), f32),
            pltpu.VMEM((wide, depth), bf16),
            pltpu.VMEM((wide, depth), bf16),
            pltpu.VMEM((DENSITIES * size, 3 * block), bf16),
            pltpu.VMEM((DENSITIES * size, 3 * block), bf16),
            pltpu.VMEM((3 * block, DENSITIES * size), bf16),
            pltpu.VMEM((3 * block, DENSITIES * size), bf16),
            pltpu.VMEM((DENSITIES, WINDOW, WINDOW), bf16),
            pltpu.VMEM((DENSITIES, WINDOW, WINDOW), bf16),
            pltpu.VMEM((DENSITIES, DENSITIES, own, depth), bf16),
            pltpu.VMEM((groups, DENSITIES * size, depth), f32),
            pltpu.VMEM((DENSITIES, own, depth), bf16),
            pltpu.VMEM((DENSITIES, own, depth), f32),
            pltpu.VMEM((DENSITIES, own, depth), bf16),
            pltpu.VMEM((DENSITIES, own, LANES), f32),
            pltpu.VMEM((groups, DENSITIES * size, depth), bf16),
            pltpu.VMEM((groups, DENSITIES * size, depth), bf16),
            pltpu.VMEM((ext_rows, ext_cols, depth), f32),
            pltpu.VMEM((ext_rows, reach, depth), f32),
            pltpu.VMEM((ext_rows, reach, depth), f32),
            pltpu.VMEM((reach, span_cols, depth), f32),
            pltpu.VMEM((reach, span_cols, depth), f32),
            pltpu.SemaphoreType.DMA((2,)),
            pltpu.SemaphoreType.DMA((chunks,)),
            pltpu.SemaphoreType.DMA((8, chunks)),
            pltpu.SemaphoreType.DMA((8, chunks)),
            pltpu.SemaphoreType.DMA((8, chunks)),
            pltpu.SemaphoreType.DMA((8, chunks)),
        ],
        compiler_params=pltpu.CompilerParams(
            vmem_limit_bytes=60 << 20, collective_id=0, has_side_effects=True),
    )(tangent, hessian.reshape(DENSITIES, DENSITIES, own, depth), kernel_rows, kernel_cols, kernel_depth)


def solution(mesh):
    return jax.shard_map(
        per_device,
        mesh=mesh,
        in_specs=(P("gx", "gy", None), P(None, None, "gx", "gy", None), P(), P(), P()),
        out_specs=P("gx", "gy", None),
        check_vma=False,
    )
```

time: 50.3 us -> 45.3 us (0.901)
  Pallas kernels: 48.3 us -> 43.2 us
    pallas_call x1, Pallas kernels: 48.3 us -> 43.2 us  [per_device(): pl.pallas_call(lambda *refs: compute(sizes, counts, *refs), out_shape=jax...]
where the time goes in v1:
time: 45.3 us; the launch traced here: 45.1 us
  Pallas kernels  43.2 us (95%)
  local copies, waits for them, and re-layouts  1.88 us (4%)
    pallas_call x1, Pallas kernels, per_device(): pl.pallas_call(lambda *refs: compute(sizes, counts, *refs), out_shape=jax...  43.2 us
    unnamed x1, local copies, waits for them, and re-layouts  1.88 us

profile of v1, /device:TPU:0, one launch (start us, length us, event | category | flops | bytes accessed | tf_op | source)
XLA Modules:
  0.0 45.1 jit_solution(5894936696257023649)
XLA Ops:
  0.0 43.2 %shard_map.55 = f32[16,16,512]{2,1,0:T(8,128)} custom-call(f32[16,16,512]{2,1,0:T(8,128)} %refs_0_.1, bf16[5,5,256,512]{3,2,1,0:T(8,128)(2,1)} %bitcast.1, f32[5,17]{1,0:T(8,128)} %refs_2_.1, f32[5,17]{1,0:T(8,128)} %refs_3_.1, bf16[5,17]{1,0:T(8,128)(2,1)} %refs_4_.1), custom_call_target="tpu_custom_call" | custom-call | tf_op jit(solution)/shard_map/pallas_call | solution.py:335
  43.2 1.9 %copy.7 = f32[16,16,512]{2,1,0:T(8,128)} copy(f32[16,16,512]{2,1,0:T(8,128)} %shard_map.55) | data formatting | bytes 1048576

commit v2 on v1

--- a/solution.py
+++ b/solution.py
@@ -142,11 +142,6 @@
         plan.append((spread.at[last, inner_cols, z], from_up.at[:, :, z], down))
         for kind, (source, target, device) in enumerate(plan):
             returns[kind, c] = remote(source, target, back_send_sems.at[kind, c], back_recv_sems.at[kind, c], device)
-    for c in range(chunks):
-        for kind in range(4):
-            copies[kind, c].start()
-    fetch.start()
-
     def relay(c):
         for kind in (0, 1):
             copies[kind, c].wait_recv()
@@ -213,7 +208,7 @@
                     lowered[a, at, z] = total.astype(jnp.bfloat16)
             return carry
 
-        lax.fori_loop(0, own // step, piece, 0)
+        lax.fori_loop(0, own // step, piece, 0, unroll=4)
 
     def against_depth(k):
         z, here, ahead = pl.ds(k * LANES, WINDOW), lanes[k], lanes[k + 1]
@@ -277,47 +272,60 @@
         top, bottom = pl.ds(reach, reach), pl.ds(span_rows, reach)
         spread[top, inner_cols, z] = spread[top, inner_cols, z] + from_up[:, :, z]
         spread[bottom, inner_cols, z] = spread[bottom, inner_cols, z] + from_down[:, :, z]
-        copy = pltpu.make_async_copy(spread.at[inner_rows, inner_cols, z], out_ref.at[:, :, z], out_sems.at[c])
-        copy.start()
-        return copy
-
+        out_ref[:, :, z] = spread[inner_rows, inner_cols, z]
+
+    copies[0, 0].start()
+    copies[1, 0].start()
+    copies[2, 0].start()
+    copies[3, 0].start()
+    copies[0, 1].start()
+    copies[1, 1].start()
+    copies[2, 1].start()
+    copies[3, 1].start()
+    copies[2, 2].start()
+    copies[3, 2].start()
+    copies[2, 3].start()
+    copies[3, 3].start()
+    fetch.start()
     rows, cols = rows_ref[...], cols_ref[...]
     build_forward(sizes, rows, cols, fwd_high, fwd_low)
     build_bands(depth_ref[...].astype(jnp.float32), band, band_t)
     build_backward(sizes, rows, cols, bwd_high, bwd_low)
     home.wait()
     relay(0)
+    copies[0, 2].start()
+    copies[1, 2].start()
     middle(0, 2)
     relay(1)
-    for c in range(2, chunks, 2):
-        middle(c, min(c + 2, chunks))
+    copies[0, 3].start()
+    copies[1, 3].start()
+    middle(2, 4)
     edges(0, 2)
-    relayed = 2
     fetch.wait()
-    for k in range(chunks - 1):
-        if k > 0:
-            edges(k + 1, k + 2)
-        if relayed < chunks:
-            relay(relayed)
-            relayed += 1
-        along_depth(k)
-        gradient(k)
-        if k > 0:
-            strips(k - 1)
-        against_depth(k)
-        final_step = k == chunks - 2
-        corners(k, chunks if final_step else k + 1)
-        if relayed < chunks:
-            relay(relayed)
-            relayed += 1
-        sides(k, chunks if final_step else k + 1)
-    strips(chunks - 2)
-    strips(chunks - 1)
+    relay(2)
+    along_depth(0)
+    gradient(0)
+    against_depth(0)
+    corners(0, 1)
+    relay(3)
+    edges(2, 3)
+    along_depth(1)
+    gradient(1)
+    against_depth(1)
+    corners(1, 2)
+    strips(0)
+    edges(3, 4)
+    along_depth(2)
+    gradient(2)
+    against_depth(2)
+    corners(2, 4)
+    strips(1)
+    sides(0, 4)
+    strips(2)
+    strips(3)
     outs = [final(c) for c in range(chunks)]
     for copy in list(copies.values()) + list(returns.values()):
         copy.wait_send()
-    for copy in outs:
-        copy.wait()
 
 
 def per_device(tangent, hessian, kernel_rows, kernel_cols, kernel_depth):
@@ -334,9 +342,9 @@
     bf16, f32 = jnp.bfloat16, jnp.float32
     return pl.pallas_call(
         lambda *refs: compute(sizes, counts, *refs),
-        out_shape=jax.ShapeDtypeStruct((span_rows, span_cols, depth), f32),
+        out_shape=pltpu.VMEM((span_rows, span_cols, depth), f32),
         in_specs=[anywhere, anywhere, full, full, full],
-        out_specs=anywhere,
+        out_specs=full,
         scratch_shapes=[
             pltpu.VMEM((ext_rows, ext_cols, depth), f32),
             pltpu.VMEM((wide, depth), bf16),

time: 45.3 us -> 40.6 us (0.90)
  Pallas kernels: 43.2 us -> 39.6 us
  local copies, waits for them, and re-layouts: 1.88 us -> 0.8 us
    pallas_call x1, Pallas kernels: 43.2 us -> 39.6 us  [per_device(): pl.pallas_call(lambda *refs: compute(sizes, counts, *refs), out_shape=plt...]
    unnamed x1, local copies, waits for them, and re-layouts: 1.88 us -> 0.8 us
where the time goes in v2:
time: 40.6 us; the launch traced here: 40.4 us
  Pallas kernels  39.6 us (98%)
  local copies, waits for them, and re-layouts  0.8 us (2%)
    pallas_call x1, Pallas kernels, per_device(): pl.pallas_call(lambda *refs: compute(sizes, counts, *refs), out_shape=plt...  39.6 us

profile of v2, /device:TPU:0, one launch (start us, length us, event | category | flops | bytes accessed | tf_op | source)
XLA Modules:
  0.0 40.4 jit_solution(5810844020545689084)
XLA Ops:
  0.0 39.6 %shard_map.55 = f32[16,16,512]{2,1,0:T(8,128)S(1)} custom-call(f32[16,16,512]{2,1,0:T(8,128)} %refs_0_.1, bf16[5,5,256,512]{3,2,1,0:T(8,128)(2,1)} %bitcast.1, f32[5,17]{1,0:T(8,128)} %refs_2_.1, f32[5,17]{1,0:T(8,128)} %refs_3_.1, bf16[5,17]{1,0:T(8,128)(2,1)} %refs_4_.1), custom_call_target="tpu_custom_call" | custom-call | tf_op jit(solution)/shard_map/pallas_call | solution.py:343
  39.6 0.8 %copy.7 = f32[16,16,512]{2,1,0:T(8,128)} copy(f32[16,16,512]{2,1,0:T(8,128)S(1)} %shard_map.55) | data formatting | bytes 1048576

commit v3 on v1

v3 whole, which is shorter than its diff:
```python
import jax
import jax.numpy as jnp
from jax import lax
from jax.experimental import pallas as pl
from jax.experimental.pallas import tpu as pltpu
from jax.sharding import PartitionSpec as P

RADIUS = 8
DENSITIES = 5
TAPS = 2 * RADIUS + 1
LANES = 128
WINDOW = 2 * LANES


def split(value):
    high = value.astype(jnp.bfloat16)
    low = (value - high.astype(jnp.float32)).astype(jnp.bfloat16)
    return high, low


def dot(left, right):
    return jnp.dot(left, right, preferred_element_type=jnp.float32)


def dot3(left_high, left_low, right_high, right_low):
    return dot(left_high, right_high) + dot(left_high, right_low) + dot(left_low, right_high)


def picked(taps, index):
    total = jnp.zeros(index.shape, jnp.float32)
    for tap in range(TAPS):
        weight = jnp.broadcast_to(taps[:, tap : tap + 1], index.shape)
        total = jnp.where(index == tap, weight, total)
    return total


def iota(shape, axis):
    return lax.broadcasted_iota(jnp.int32, shape, axis)


def build_forward(sizes, rows, cols, high_ref, low_ref):
    span_cols, ext_cols = sizes[1], sizes[3]
    wide = 3 * RADIUS * ext_cols
    row_index = iota((RADIUS, wide), 1) // ext_cols - iota((RADIUS, wide), 0)
    col_index = iota((span_cols, LANES), 1) % ext_cols - iota((span_cols, LANES), 0)
    for a in range(DENSITIES):
        by_row = picked(rows[a : a + 1], row_index)
        by_col = picked(cols[a : a + 1], col_index)
        by_col = jnp.concatenate([by_col] * (wide // LANES), axis=1)
        for r in range(RADIUS):
            at = pl.ds((a * RADIUS + r) * span_cols, span_cols)
            high_ref[at, :], low_ref[at, :] = split(by_row[r : r + 1, :] * by_col)


def build_backward(sizes, rows, cols, high_ref, low_ref):
    span_cols, ext_cols = sizes[1], sizes[3]
    size = RADIUS * span_cols
    row_index = iota((3 * RADIUS, size), 0) - iota((3 * RADIUS, size), 1) // span_cols
    col_index = iota((ext_cols, size), 0) - iota((ext_cols, size), 1) % span_cols
    for a in range(DENSITIES):
        by_row = picked(rows[a : a + 1], row_index)
        by_col = picked(cols[a : a + 1], col_index)
        into = pl.ds(a * size, size)
        for r in range(3 * RADIUS):
            at = pl.ds(r * ext_cols, ext_cols)
            high_ref[at, into], low_ref[at, into] = split(by_row[r : r + 1, :] * by_col)


def build_bands(depth_taps, band_ref, band_t_ref):
    step = 16
    shape = (step, WINDOW)
    offset = iota(shape, 0) - iota(shape, 1)
    for a in range(DENSITIES):
        taps = depth_taps[a : a + 1]
        for ref, sign in ((band_ref, 1), (band_t_ref, -1)):
            middle = picked(taps, sign * (offset + LANES) + RADIUS)
            for i in range(WINDOW // step):
                value = pltpu.roll(middle, (step * i - LANES) % WINDOW, 1)
                if i in (0, WINDOW // step - 1):
                    value = jnp.where(jnp.abs(offset + step * i) <= RADIUS, value, 0.0)
                ref[a, pl.ds(i * step, step), :] = value.astype(jnp.bfloat16)


def compute(sizes, counts, tangent_ref, hess_ref, rows_ref, cols_ref, depth_ref, out_ref,
            ext, high, low, fwd_high, fwd_low, bwd_high, bwd_low, band, band_t, hess,
            acc, lateral, dens, lowered, pending, back_high, back_low, spread,
            from_left, from_right, from_ring,
            local_sems, send_sems, recv_sems, back_send_sems, back_recv_sems):
    span_rows, span_cols, ext_rows, ext_cols = sizes
    depth = acc.shape[-1]
    reach = RADIUS
    groups = span_rows // reach
    own, size, block = span_rows * span_cols, reach * span_cols, reach * ext_cols
    chunks = depth // LANES
    gx, gy = lax.axis_index("gx"), lax.axis_index("gy")
    left = {"gy": lax.rem(gy + counts[1] - 1, counts[1])}
    right = {"gy": lax.rem(gy + 1, counts[1])}
    mesh_ids = pl.DeviceIdType.MESH

    inner_rows, inner_cols = pl.ds(reach, span_rows), pl.ds(reach, span_cols)
    barrier = pltpu.get_barrier_semaphore()
    rings = [{"gx": lax.rem(gx + counts[0] + step, counts[0])} for step in (-1, 1)]
    for neighbour in (*rings, left, right):
        pl.semaphore_signal(barrier, inc=1, device_id=neighbour, device_id_type=mesh_ids)
    fetch = pltpu.make_async_copy(hess_ref, hess, local_sems.at[0])
    home = pltpu.make_async_copy(tangent_ref, ext.at[inner_rows, inner_cols, :], local_sems.at[1])
    home.start()
    pl.semaphore_wait(barrier, 4)

    first_cols, last_cols = pl.ds(0, reach), pl.ds(reach + span_cols, reach)
    near_first, near_last = pl.ds(reach, reach), pl.ds(span_cols, reach)
    lanes = [pl.ds(c * LANES, LANES) for c in range(chunks)]

    def remote(source, target, send_sem, recv_sem, device):
        return pltpu.make_async_remote_copy(
            src_ref=source, dst_ref=target, send_sem=send_sem, recv_sem=recv_sem,
            device_id=device, device_id_type=mesh_ids)

    head_cols, tail_cols = pl.ds(0, reach), pl.ds(span_cols - reach, reach)
    every_row, every_col = pl.ds(0, span_rows), pl.ds(0, span_cols)
    copies, returns = {}, {}
    for c, z in enumerate(lanes):
        plan = [
            (tangent_ref.at[every_row, tail_cols, z], ext.at[inner_rows, first_cols, z], right),
            (tangent_ref.at[every_row, head_cols, z], ext.at[inner_rows, last_cols, z], left),
        ]
        for side, (source, target, device) in enumerate(plan):
            copies[2 + side, c] = remote(source, target, send_sems.at[2 + side, c], recv_sems.at[2 + side, c], device)
        plan = [
            (spread.at[inner_rows, last_cols, z], from_left.at[inner_rows, :, z], right),
            (spread.at[inner_rows, first_cols, z], from_right.at[inner_rows, :, z], left),
        ]
        for side, (source, target, device) in enumerate(plan):
            returns[4 + side, c] = remote(source, target, back_send_sems.at[4 + side, c], back_recv_sems.at[4 + side, c], device)

    odd = lax.rem(gx, 2)
    FAR, NEAR = odd, 1 - odd

    def ring(group):
        return {"gx": lax.rem(gx + counts[0] - 1 + 2 * group, counts[0])}

    def halo(group):
        return pl.ds(group * (reach + span_rows), reach)

    def halo_copy(group, c):
        z = lanes[c]
        source = tangent_ref.at[pl.ds(group * (span_rows - reach), reach), every_col, z]
        return remote(source, ext.at[halo(1 - group), inner_cols, z], send_sems.at[1 - group, c], recv_sems.at[1 - group, c], ring(group))

    def corner_copies(group, c):
        z, rows_at = lanes[c], halo(group)
        for side, near, far, device in ((0, near_last, first_cols, right), (1, near_first, last_cols, left)):
            kind = 4 + 2 * group + side
            yield remote(ext.at[rows_at, near, z], ext.at[rows_at, far, z], send_sems.at[kind, c], recv_sems.at[kind, c], device)

    def return_copies(group, c):
        z, rows_at = lanes[c], halo(group)
        for side, cols_at, target, device in ((0, last_cols, from_left, right), (1, first_cols, from_right, left)):
            kind = 2 * group + side
            yield remote(spread.at[rows_at, cols_at, z], target.at[rows_at, :, z], back_send_sems.at[kind, c], back_recv_sems.at[kind, c], device)

    def strip_copy(group, c):
        z, kind = lanes[c], 6 + group
        return remote(spread.at[halo(group), inner_cols, z], from_ring.at[1 - group, :, :, z], back_send_sems.at[kind, c], back_recv_sems.at[kind, c], ring(group))

    def launch(*pairs):
        for kind, c in pairs:
            copies[kind, c].start()

    def relay(group, c):
        halo_copy(1 - group, c).wait_recv()
        for copy in corner_copies(group, c):
            copy.start()

    def at_lanes(begin, end):
        return pl.ds(begin * LANES, (end - begin) * LANES)

    def prepare(z, start, count):
        value = ext[pl.ds(start, count), :, z].reshape(count * ext_cols, z.size)
        at = pl.ds(start * ext_cols, count * ext_cols)
        high[at, z], low[at, z] = split(value)

    def middle(begin, end):
        z = at_lanes(begin, end)
        for c in range(begin, end):
            copies[2, c].wait_recv()
            copies[3, c].wait_recv()
        prepare(z, reach, span_rows)
        data = pl.ds(block, 2 * block)
        for group in (0, 1):
            weights = pl.ds((1 - group) * block, 2 * block)
            acc[group, :, z] = dot3(fwd_high[:, weights], fwd_low[:, weights], high[data, z], low[data, z])

    def arrived(group, begin, end):
        for c in range(begin, end):
            for copy in corner_copies(group, c):
                copy.wait_recv()

    def edges(group, begin, end):
        def emit():
            z = at_lanes(begin, end)
            prepare(z, group * (reach + span_rows), reach)
            weights, data = pl.ds(group * 2 * block, block), pl.ds(group * 3 * block, block)
            total = acc[group, :, z] + dot3(fwd_high[:, weights], fwd_low[:, weights], high[data, z], low[data, z])
            lateral[group, :, z] = total.astype(jnp.bfloat16)

        return [emit]

    keep = iota((size, LANES), 1) < LANES // 2

    def along_depth(group, k):
        z, here, ahead = pl.ds(k * LANES, WINDOW), lanes[k], lanes[k + 1]

        def emit(a):
            part = pl.ds(a * size, size)
            value = dot(lateral[group, part, z], band[a])
            begin = value[:, :LANES]
            dens[group, part, here] = begin if k == 0 else jnp.where(keep, dens[group, part, here], begin)
            dens[group, part, ahead] = value[:, LANES:]

        return [lambda a=a: emit(a) for a in range(DENSITIES)]

    def gradient(group, k):
        step = 16

        def emit(r, z):
            at = pl.ds(group * size + r * step, step)
            values = [dens[group, pl.ds(b * size + r * step, step), z] for b in range(DENSITIES)]
            for a in range(DENSITIES):
                total = None
                for b in range(DENSITIES):
                    term = hess[a, b, at, z].astype(jnp.float32) * values[b]
                    total = term if total is None else total + term
                lowered[group, pl.ds(a * size + r * step, step), z] = total.astype(jnp.bfloat16)

        return [lambda r=r, z=z: emit(r, z) for r in range(size // step) for z in (lanes[k], lanes[k + 1])]

    def against_depth(group, k):
        z, here, ahead = pl.ds(k * LANES, WINDOW), lanes[k], lanes[k + 1]

        def emit(a):
            part = pl.ds(a * size, size)
            value = dot(lowered[group, part, z], band_t[a])
            begin, rest = value[:, :LANES], value[:, LANES:]
            if k > 0:
                begin = jnp.where(keep, pending[group, part, :], begin)
            back_high[group, part, here], back_low[group, part, here] = split(begin)
            if k == chunks - 2:
                back_high[group, part, ahead], back_low[group, part, ahead] = split(rest)
            else:
                pending[group, part, :] = rest

        return [lambda a=a: emit(a) for a in range(DENSITIES)]

    def corners(group, begin, end):
        def emit():
            z = at_lanes(begin, end)
            part = pl.ds(group * 2 * block, block)
            value = dot3(bwd_high[part, :], bwd_low[part, :], back_high[group, :, z], back_low[group, :, z])
            spread[halo(group), :, z] = value.reshape(reach, ext_cols, z.size)

        return [emit]

    def send_corners(group, begin, end):
        for c in range(begin, end):
            for copy in return_copies(group, c):
                copy.start()

    def sides(begin, end):
        z = at_lanes(begin, end)
        for index in (0, 1):
            total = None
            for group in (0, 1):
                part = pl.ds((1 + index - group) * block, block)
                term = dot3(bwd_high[part, :], bwd_low[part, :], back_high[group, :, z], back_low[group, :, z])
                total = term if total is None else total + term
            spread[pl.ds((1 + index) * reach, reach), :, z] = total.reshape(reach, ext_cols, z.size)
        for c in range(begin, end):
            for kind in (4, 5):
                returns[kind, c].start()

    def strips(group, c):
        z, rows_at = lanes[c], halo(group)
        for copy in return_copies(group, c):
            copy.wait_recv()
        spread[rows_at, near_first, z] = spread[rows_at, near_first, z] + from_left[rows_at, :, z]
        spread[rows_at, near_last, z] = spread[rows_at, near_last, z] + from_right[rows_at, :, z]
        strip_copy(group, c).start()

    def final(c):
        z = lanes[c]
        for kind in (4, 5):
            returns[kind, c].wait_recv()
        spread[inner_rows, near_first, z] = spread[inner_rows, near_first, z] + from_left[inner_rows, :, z]
        spread[inner_rows, near_last, z] = spread[inner_rows, near_last, z] + from_right[inner_rows, :, z]
        for group in (0, 1):
            strip_copy(1 - group, c).wait_recv()
            edge, rows_at = pl.ds(reach + group * reach, reach), pl.ds(group * reach, reach)
            out_ref[rows_at, :, z] = spread[edge, inner_cols, z] + from_ring[group, :, :, z]

    def mix(*streams):
        order = sorted(((n + 0.5) / len(stream), m, n) for m, stream in enumerate(streams) for n in range(len(stream)))
        for _, m, n in order:
            streams[m][n]()

    halo_copy(FAR, 0).start()
    halo_copy(NEAR, 0).start()
    launch((2, 0), (3, 0))
    halo_copy(FAR, 1).start()
    halo_copy(NEAR, 1).start()
    launch((2, 1), (3, 1))
    launch((2, 2), (3, 2))
    launch((2, 3), (3, 3))
    fetch.start()
    rows, cols = rows_ref[...], cols_ref[...]
    build_forward(sizes, rows, cols, fwd_high, fwd_low)
    build_bands(depth_ref[...].astype(jnp.float32), band, band_t)
    build_backward(sizes, rows, cols, bwd_high, bwd_low)
    home.wait()
    relay(FAR, 0)
    relay(NEAR, 0)
    halo_copy(FAR, 2).start()
    halo_copy(NEAR, 2).start()
    middle(0, 2)
    relay(FAR, 1)
    relay(NEAR, 1)
    halo_copy(FAR, 3).start()
    halo_copy(NEAR, 3).start()
    middle(2, 4)
    fetch.wait()
    arrived(FAR, 0, 2)
    arrived(NEAR, 0, 2)
    mix(edges(0, 0, 2))
    mix(edges(1, 0, 2))
    relay(FAR, 2)
    relay(NEAR, 2)
    mix(along_depth(0, 0))
    mix(along_depth(1, 0))
    mix(gradient(0, 0))
    mix(gradient(1, 0))
    mix(against_depth(0, 0))
    mix(against_depth(1, 0))
    mix(corners(0, 0, 1))
    mix(corners(1, 0, 1))
    send_corners(FAR, 0, 1)
    send_corners(NEAR, 0, 1)
    relay(FAR, 3)
    relay(NEAR, 3)
    arrived(FAR, 2, 3)
    arrived(NEAR, 2, 3)
    mix(edges(0, 2, 3))
    mix(edges(1, 2, 3))
    mix(along_depth(0, 1))
    mix(along_depth(1, 1))
    mix(gradient(0, 1))
    mix(gradient(1, 1))
    mix(against_depth(0, 1))
    mix(against_depth(1, 1))
    mix(corners(0, 1, 2))
    mix(corners(1, 1, 2))
    send_corners(FAR, 1, 2)
    send_corners(NEAR, 1, 2)
    strips(FAR, 0)
    strips(NEAR, 0)
    arrived(FAR, 3, 4)
    arrived(NEAR, 3, 4)
    mix(edges(0, 3, 4))
    mix(edges(1, 3, 4))
    mix(along_depth(0, 2))
    mix(along_depth(1, 2))
    mix(gradient(0, 2))
    mix(gradient(1, 2))
    mix(against_depth(0, 2))
    mix(against_depth(1, 2))
    mix(corners(0, 2, 4))
    mix(corners(1, 2, 4))
    send_corners(FAR, 2, 4)
    send_corners(NEAR, 2, 4)
    strips(FAR, 1)
    strips(NEAR, 1)
    sides(0, 2)
    strips(FAR, 2)
    strips(NEAR, 2)
    strips(FAR, 3)
    strips(NEAR, 3)
    sides(2, 4)
    final(0)
    final(1)
    final(2)
    final(3)
    for copy in list(copies.values()) + list(returns.values()):
        copy.wait_send()
    for c in range(chunks):
        for group in (0, 1):
            halo_copy(group, c).wait_send()
            strip_copy(group, c).wait_send()
            for copy in (*corner_copies(group, c), *return_copies(group, c)):
                copy.wait_send()


def per_device(tangent, hessian, kernel_rows, kernel_cols, kernel_depth):
    span_rows, span_cols, depth = tangent.shape
    reach = RADIUS
    ext_rows, ext_cols = span_rows + 2 * reach, span_cols + 2 * reach
    sizes = (span_rows, span_cols, ext_rows, ext_cols)
    counts = (lax.axis_size("gx"), lax.axis_size("gy"))
    own, wide = span_rows * span_cols, ext_rows * ext_cols
    groups, size, block = span_rows // reach, reach * span_cols, reach * ext_cols
    chunks = depth // LANES
    assert groups == 2 and chunks > 1 and counts[0] % 2 == 0
    full = pl.BlockSpec(memory_space=pltpu.VMEM)
    anywhere = pl.BlockSpec(memory_space=pl.ANY)
    bf16, f32 = jnp.bfloat16, jnp.float32
    return pl.pallas_call(
        lambda *refs: compute(sizes, counts, *refs),
        out_shape=pltpu.VMEM((span_rows, span_cols, depth), f32),
        in_specs=[anywhere, anywhere, full, full, full],
        out_specs=full,
        scratch_shapes=[
            pltpu.VMEM((ext_rows, ext_cols, depth), f32),
            pltpu.VMEM((wide, depth), bf16),
            pltpu.VMEM((wide, depth), bf16),
            pltpu.VMEM((DENSITIES * size, 3 * block), bf16),
            pltpu.VMEM((DENSITIES * size, 3 * block), bf16),
            pltpu.VMEM((3 * block, DENSITIES * size), bf16),
            pltpu.VMEM((3 * block, DENSITIES * size), bf16),
            pltpu.VMEM((DENSITIES, WINDOW, WINDOW), bf16),
            pltpu.VMEM((DENSITIES, WINDOW, WINDOW), bf16),
            pltpu.VMEM((DENSITIES, DENSITIES, own, depth), bf16),
            pltpu.VMEM((groups, DENSITIES * size, depth), f32),
            pltpu.VMEM((groups, DENSITIES * size, depth), bf16),
            pltpu.VMEM((groups, DENSITIES * size, depth), f32),
            pltpu.VMEM((groups, DENSITIES * size, depth), bf16),
            pltpu.VMEM((groups, DENSITIES * size, LANES), f32),
            pltpu.VMEM((groups, DENSITIES * size, depth), bf16),
            pltpu.VMEM((groups, DENSITIES * size, depth), bf16),
            pltpu.VMEM((ext_rows, ext_cols, depth), f32),
            pltpu.VMEM((ext_rows, reach, depth), f32),
            pltpu.VMEM((ext_rows, reach, depth), f32),
            pltpu.VMEM((2, reach, span_cols, depth), f32),
            pltpu.SemaphoreType.DMA((2,)),
            pltpu.SemaphoreType.DMA((8, chunks)),
            pltpu.SemaphoreType.DMA((8, chunks)),
            pltpu.SemaphoreType.DMA((8, chunks)),
            pltpu.SemaphoreType.DMA((8, chunks)),
        ],
        compiler_params=pltpu.CompilerParams(
            vmem_limit_bytes=60 << 20, collective_id=0, has_side_effects=True),
    )(tangent, hessian.reshape(DENSITIES, DENSITIES, own, depth), kernel_rows, kernel_cols, kernel_depth)


def solution(mesh):
    return jax.shard_map(
        per_device,
        mesh=mesh,
        in_specs=(P("gx", "gy", None), P(None, None, "gx", "gy", None), P(), P(), P()),
        out_specs=P("gx", "gy", None),
        check_vma=False,
    )
```

time: 45.3 us -> 39.4 us (0.87)
  Pallas kernels: 43.2 us -> 38.4 us
  local copies, waits for them, and re-layouts: 1.88 us -> 0.8 us
    pallas_call x1, Pallas kernels: 43.2 us -> 38.4 us  [per_device(): pl.pallas_call(lambda *refs: compute(sizes, counts, *refs), out_shape=plt...]
    unnamed x1, local copies, waits for them, and re-layouts: 1.88 us -> 0.8 us
where the time goes in v3:
time: 39.4 us; the launch traced here: 39.2 us
  Pallas kernels  38.4 us (97%)
  local copies, waits for them, and re-layouts  0.8 us (2%)
    pallas_call x1, Pallas kernels, per_device(): pl.pallas_call(lambda *refs: compute(sizes, counts, *refs), out_shape=plt...  38.4 us
    unnamed x1, local copies, waits for them, and re-layouts  0.8 us

profile of v3, /device:TPU:0, one launch (start us, length us, event | category | flops | bytes accessed | tf_op | source)
XLA Modules:
  0.0 39.2 jit_solution(12076596054384739659)
XLA Ops:
  0.0 38.4 %shard_map.55 = f32[16,16,512]{2,1,0:T(8,128)S(1)} custom-call(f32[16,16,512]{2,1,0:T(8,128)} %refs_0_.1, bf16[5,5,256,512]{3,2,1,0:T(8,128)(2,1)} %bitcast.1, f32[5,17]{1,0:T(8,128)} %refs_2_.1, f32[5,17]{1,0:T(8,128)} %refs_3_.1, bf16[5,17]{1,0:T(8,128)(2,1)} %refs_4_.1), custom_call_target="tpu_custom_call" | custom-call | tf_op jit(solution)/shard_map/pallas_call | solution.py:414
  38.4 0.8 %copy.7 = f32[16,16,512]{2,1,0:T(8,128)} copy(f32[16,16,512]{2,1,0:T(8,128)S(1)} %shard_map.55) | data formatting | bytes 1048576

commit v4 on v3

--- a/solution.py
+++ b/solution.py
@@ -81,10 +81,10 @@
                 ref[a, pl.ds(i * step, step), :] = value.astype(jnp.bfloat16)
 
 
-def compute(sizes, counts, tangent_ref, hess_ref, rows_ref, cols_ref, depth_ref, out_ref,
+def compute(sizes, counts, tangent_ref, hess_ref, rows_hbm, cols_hbm, depth_hbm, out_ref,
             ext, high, low, fwd_high, fwd_low, bwd_high, bwd_low, band, band_t, hess,
             acc, lateral, dens, lowered, pending, back_high, back_low, spread,
-            from_left, from_right, from_ring,
+            from_left, from_right, from_ring, rows_ref, cols_ref, depth_ref,
             local_sems, send_sems, recv_sems, back_send_sems, back_recv_sems):
     span_rows, span_cols, ext_rows, ext_cols = sizes
     depth = acc.shape[-1]
@@ -105,6 +105,10 @@
     fetch = pltpu.make_async_copy(hess_ref, hess, local_sems.at[0])
     home = pltpu.make_async_copy(tangent_ref, ext.at[inner_rows, inner_cols, :], local_sems.at[1])
     home.start()
+    factors = [pltpu.make_async_copy(source, target, local_sems.at[2 + n]) for n, (source, target) in enumerate(
+        ((rows_hbm, rows_ref), (cols_hbm, cols_ref), (depth_hbm, depth_ref)))]
+    for copy in factors:
+        copy.start()
     pl.semaphore_wait(barrier, 4)
 
     first_cols, last_cols = pl.ds(0, reach), pl.ds(reach + span_cols, reach)
@@ -312,6 +316,8 @@
     launch((2, 2), (3, 2))
     launch((2, 3), (3, 3))
     fetch.start()
+    for copy in factors:
+        copy.wait()
     rows, cols = rows_ref[...], cols_ref[...]
     build_forward(sizes, rows, cols, fwd_high, fwd_low)
     build_bands(depth_ref[...].astype(jnp.float32), band, band_t)
@@ -321,31 +327,31 @@
     relay(NEAR, 0)
     halo_copy(FAR, 2).start()
     halo_copy(NEAR, 2).start()
+    halo_copy(FAR, 3).start()
+    halo_copy(NEAR, 3).start()
     middle(0, 2)
     relay(FAR, 1)
     relay(NEAR, 1)
-    halo_copy(FAR, 3).start()
-    halo_copy(NEAR, 3).start()
     middle(2, 4)
     fetch.wait()
     arrived(FAR, 0, 2)
     arrived(NEAR, 0, 2)
+    relay(FAR, 2)
+    relay(NEAR, 2)
     mix(edges(0, 0, 2))
     mix(edges(1, 0, 2))
-    relay(FAR, 2)
-    relay(NEAR, 2)
     mix(along_depth(0, 0))
     mix(along_depth(1, 0))
     mix(gradient(0, 0))
     mix(gradient(1, 0))
     mix(against_depth(0, 0))
     mix(against_depth(1, 0))
+    relay(FAR, 3)
+    relay(NEAR, 3)
     mix(corners(0, 0, 1))
     mix(corners(1, 0, 1))
     send_corners(FAR, 0, 1)
     send_corners(NEAR, 0, 1)
-    relay(FAR, 3)
-    relay(NEAR, 3)
     arrived(FAR, 2, 3)
     arrived(NEAR, 2, 3)
     mix(edges(0, 2, 3))
@@ -414,7 +420,7 @@
     return pl.pallas_call(
         lambda *refs: compute(sizes, counts, *refs),
         out_shape=pltpu.VMEM((span_rows, span_cols, depth), f32),
-        in_specs=[anywhere, anywhere, full, full, full],
+        in_specs=[anywhere] * 5,
         out_specs=full,
         scratch_shapes=[
             pltpu.VMEM((ext_rows, ext_cols, depth), f32),
@@ -438,7 +444,10 @@
             pltpu.VMEM((ext_rows, reach, depth), f32),
             pltpu.VMEM((ext_rows, reach, depth), f32),
             pltpu.VMEM((2, reach, span_cols, depth), f32),
-            pltpu.SemaphoreType.DMA((2,)),
+            pltpu.VMEM(kernel_rows.shape, f32),
+            pltpu.VMEM(kernel_cols.shape, f32),
+            pltpu.VMEM(kernel_depth.shape, bf16),
+            pltpu.SemaphoreType.DMA((5,)),
             pltpu.SemaphoreType.DMA((8, chunks)),
             pltpu.SemaphoreType.DMA((8, chunks)),
             pltpu.SemaphoreType.DMA((8, chunks)),

time: 39.4 us -> 38.3 us (0.972)
  Pallas kernels: 38.4 us -> 37.3 us
    pallas_call x1, Pallas kernels: 38.4 us -> 37.3 us  [per_device(): pl.pallas_call(lambda *refs: compute(sizes, counts, *refs), out_shape=plt...]
where the time goes in v4:
time: 38.3 us; the launch traced here: 38.1 us
  Pallas kernels  37.3 us (97%)
  local copies, waits for them, and re-layouts  0.8 us (2%)
    pallas_call x1, Pallas kernels, per_device(): pl.pallas_call(lambda *refs: compute(sizes, counts, *refs), out_shape=plt...  37.3 us
    unnamed x1, local copies, waits for them, and re-layouts  0.8 us

profile of v4, /device:TPU:0, one launch (start us, length us, event | category | flops | bytes accessed | tf_op | source)
XLA Modules:
  0.0 38.1 jit_solution(2891175923798328379)
XLA Ops:
  0.0 37.3 %shard_map.55 = f32[16,16,512]{2,1,0:T(8,128)S(1)} custom-call(f32[16,16,512]{2,1,0:T(8,128)} %refs_0_.1, bf16[5,5,256,512]{3,2,1,0:T(8,128)(2,1)} %bitcast.1, f32[5,17]{1,0:T(8,128)} %refs_2_.1, f32[5,17]{1,0:T(8,128)} %refs_3_.1, bf16[5,17]{1,0:T(8,128)(2,1)} %refs_4_.1), custom_call_target="tpu_custom_call" | custom-call | tf_op jit(solution)/shard_map/pallas_call | solution.py:420
  37.3 0.8 %copy.7 = f32[16,16,512]{2,1,0:T(8,128)} copy(f32[16,16,512]{2,1,0:T(8,128)S(1)} %shard_map.55) | data formatting | bytes 1048576

commit v5 on v4

--- a/solution.py
+++ b/solution.py
@@ -344,10 +344,10 @@
     mix(along_depth(1, 0))
     mix(gradient(0, 0))
     mix(gradient(1, 0))
+    relay(FAR, 3)
+    relay(NEAR, 3)
     mix(against_depth(0, 0))
     mix(against_depth(1, 0))
-    relay(FAR, 3)
-    relay(NEAR, 3)
     mix(corners(0, 0, 1))
     mix(corners(1, 0, 1))
     send_corners(FAR, 0, 1)

time: 38.3 us -> 38.3 us (level)
  no operation moved by 1% of the time
where the time goes in v5:
time: 38.3 us; the launch traced here: 38.1 us
  Pallas kernels  37.3 us (97%)
  local copies, waits for them, and re-layouts  0.8 us (2%)
    pallas_call x1, Pallas kernels, per_device(): pl.pallas_call(lambda *refs: compute(sizes, counts, *refs), out_shape=plt...  37.3 us
    unnamed x1, local copies, waits for them, and re-layouts  0.8 us

profile of v5, /device:TPU:0, one launch (start us, length us, event | category | flops | bytes accessed | tf_op | source)
XLA Modules:
  0.0 38.1 jit_solution(10181011868482301463)
XLA Ops:
  0.0 37.3 %shard_map.55 = f32[16,16,512]{2,1,0:T(8,128)S(1)} custom-call(f32[16,16,512]{2,1,0:T(8,128)} %refs_0_.1, bf16[5,5,256,512]{3,2,1,0:T(8,128)(2,1)} %bitcast.1, f32[5,17]{1,0:T(8,128)} %refs_2_.1, f32[5,17]{1,0:T(8,128)} %refs_3_.1, bf16[5,17]{1,0:T(8,128)(2,1)} %refs_4_.1), custom_call_target="tpu_custom_call" | custom-call | tf_op jit(solution)/shard_map/pallas_call | solution.py:420
  37.3 0.8 %copy.7 = f32[16,16,512]{2,1,0:T(8,128)} copy(f32[16,16,512]{2,1,0:T(8,128)S(1)} %shard_map.55) | data formatting | bytes 1048576
